TPU v7x, 256 devices: a whole 4x4x8 slice. The times are simulated.
256 devices in a mesh: ctx: 8 (over x, core), head: 32 (over y, z).
Axes of the slice: x: 4, y: 4, z: 8, core: 2. Of those that a mesh axis runs over, the one named last changes fastest.
Arguments:
- queries: bfloat16 [4096, 64, 128], P('ctx', 'head'), may hold values from -42 to 42
- cached_keys: bfloat16 [4, 32768, 128], P(None, 'ctx'), may hold values from -5 to 5
- cached_values: bfloat16 [4, 32768, 128], P(None, 'ctx'), may hold values from -6 to 6
- grad_out: bfloat16 [4096, 64, 128], P('ctx', 'head'), may hold values from -96 to 96
- chosen: int32 [4, 16, 16], P(None, 'ctx'), may hold values from 0 to 511, as said below
- counts: int32 [4, 16], P(None, 'ctx'), may hold values from 8 to 16, as said below
Outputs:
- grad_query: bfloat16 [4096, 64, 128], P('ctx', 'head')
- grad_keys: bfloat16 [4, 32768, 128], P(None, ('ctx', 'head'))
- grad_values: bfloat16 [4, 32768, 128], P(None, ('ctx', 'head'))
Inputs may be any that keep to these rules, and one draw needn't show every extreme that they name: For t < counts[g, b] the entries chosen[g, b, t] are distinct; entries at t >= counts[g, b] are padding. For each group and each run of 2 query blocks starting at a multiple of 2, at most 8 live entries fall in one range of 64 blocks starting at a multiple of 64, and in every group one range receives exactly 8 from every such run. `counts`: in every group some query block has 16 live entries.
All inputs are finite; a program needn't handle non-finite values.
Results may differ from a plain program's by a relative error of at most 0.02.
Values may be sent and summed in bfloat16 or wider, within the bound.
No kernel may reach another device: no remote copies, remote signals or barrier semaphores. Data moves between devices by JAX's collectives and lax.ppermute only.
A program may use at most 64 MiB of HBM per device.

v0:
```python
import jax
import jax.numpy as jnp
from jax import lax
from jax.sharding import PartitionSpec as P

DH = 128
HPG = 16
HEAD_DEV = 2
KBS = 64
TOPB = 16
QBS = 256
QB_DEV = 2
KV_DEV = 4096
BLK_OWN = 64
CAP = 8


def body(queries, cached_keys, cached_values, grad_out, chosen, counts):
    inv_root = DH ** (-0.5)
    owners = lax.axis_size("ctx")
    head_count = lax.axis_size("head")
    per_group = HPG // HEAD_DEV
    my_group = lax.axis_index("head") // per_group
    picked = lax.dynamic_index_in_dim(chosen, my_group, 0, keepdims=False)
    live_count = lax.dynamic_index_in_dim(counts, my_group, 0, keepdims=False)
    slot_live = (jnp.arange(TOPB)[None, :] < live_count[:, None]).reshape(-1)
    flat_pick = picked.reshape(-1)
    owner_index = flat_pick // BLK_OWN
    local_index = flat_pick % BLK_OWN
    member = ((owner_index[:, None] == jnp.arange(owners)[None, :]) & slot_live[:, None]).astype(
        jnp.int32
    )
    earlier = jnp.cumsum(member, axis=0) - member
    rank_index = jnp.sum(earlier * member, axis=1)
    position = owner_index * CAP + rank_index
    target = jnp.where(slot_live, position, owners * CAP)
    requests = (
        jnp.zeros((owners * CAP,), jnp.int32)
        .at[target]
        .set(local_index, mode="drop")
        .reshape(owners, CAP)
    )
    own_keys = lax.dynamic_index_in_dim(cached_keys, my_group, 0, keepdims=False).reshape(
        BLK_OWN, KBS * DH
    )
    own_values = lax.dynamic_index_in_dim(cached_values, my_group, 0, keepdims=False).reshape(
        BLK_OWN, KBS * DH
    )
    asked_rows = lax.all_to_all(requests, "ctx", split_axis=0, concat_axis=0, tiled=True)
    key_rows = jnp.take(own_keys, asked_rows, axis=0)
    value_rows = jnp.take(own_values, asked_rows, axis=0)
    key_back = lax.all_to_all(key_rows, "ctx", split_axis=0, concat_axis=0, tiled=True)
    value_back = lax.all_to_all(value_rows, "ctx", split_axis=0, concat_axis=0, tiled=True)
    gather_at = jnp.where(slot_live, position, 0)
    selected_keys = jnp.take(key_back.reshape(owners * CAP, KBS * DH), gather_at, axis=0).reshape(
        QB_DEV, TOPB * KBS, DH
    )
    selected_values = jnp.take(
        value_back.reshape(owners * CAP, KBS * DH), gather_at, axis=0
    ).reshape(QB_DEV, TOPB * KBS, DH)
    key_live = jnp.repeat(slot_live.reshape(QB_DEV, TOPB), KBS, axis=1)
    live_mask = key_live[:, None, None, :]
    query_block_rows = queries.reshape(QB_DEV, QBS, HEAD_DEV, DH)
    block_gradients = grad_out.reshape(QB_DEV, QBS, HEAD_DEV, DH)
    logit_scores = (
        jnp.einsum(
            "eryj,ezj->eyrz", query_block_rows, selected_keys, preferred_element_type=jnp.float32
        )
        * inv_root
    )
    row_peak = jnp.max(jnp.where(live_mask, logit_scores, -jnp.inf), axis=-1, keepdims=True)
    weights_raw = jnp.where(live_mask, jnp.exp(logit_scores - row_peak), 0.0)
    weights = weights_raw / jnp.sum(weights_raw, axis=-1, keepdims=True)
    weight_halves = weights.astype(jnp.bfloat16)
    attn_out = jnp.einsum(
        "npsr,nry->nspy", weight_halves, selected_values, preferred_element_type=jnp.float32
    ).astype(jnp.bfloat16)
    attn_wide = lax.optimization_barrier(attn_out).astype(jnp.float32)
    row_dot = jnp.sum(block_gradients.astype(jnp.float32) * attn_wide, axis=-1)
    row_dot = jnp.transpose(row_dot, (0, 2, 1))[:, :, :, None]
    grad_weights = jnp.einsum(
        "eryj,ezj->eyrz", block_gradients, selected_values, preferred_element_type=jnp.float32
    )
    score_gradients = (weights * (grad_weights - row_dot) * inv_root).astype(jnp.bfloat16)
    grad_query = jnp.einsum(
        "npsr,nry->nspy", score_gradients, selected_keys, preferred_element_type=jnp.float32
    )
    grad_query = grad_query.astype(jnp.bfloat16).reshape(QB_DEV * QBS, HEAD_DEV, DH)
    slot_dk = jnp.einsum(
        "lxsi,lsxr->lir", score_gradients, query_block_rows, preferred_element_type=jnp.float32
    ).reshape(QB_DEV * TOPB, KBS * DH)
    slot_dv = jnp.einsum(
        "lxsi,lsxr->lir", weight_halves, block_gradients, preferred_element_type=jnp.float32
    ).reshape(QB_DEV * TOPB, KBS * DH)
    home_dk = (
        jnp.zeros((owners * CAP, KBS * DH), jnp.float32)
        .at[target]
        .set(slot_dk, mode="drop")
        .reshape(owners, CAP, KBS * DH)
    )
    home_dv = (
        jnp.zeros((owners * CAP, KBS * DH), jnp.float32)
        .at[target]
        .set(slot_dv, mode="drop")
        .reshape(owners, CAP, KBS * DH)
    )
    block_match = (asked_rows.reshape(-1)[None, :] == jnp.arange(BLK_OWN)[:, None]).astype(
        jnp.float32
    )
    groups = head_count // per_group
    group_onehot = (jnp.arange(groups) == my_group).astype(jnp.float32)
    recv_dk, recv_dv = (
        lax.all_to_all(
            home_dk.astype(jnp.bfloat16), "ctx", split_axis=0, concat_axis=0, tiled=True
        ).astype(home_dk.dtype),
        lax.all_to_all(
            home_dv.astype(jnp.bfloat16), "ctx", split_axis=0, concat_axis=0, tiled=True
        ).astype(home_dv.dtype),
    )
    total_dk = jnp.dot(
        block_match,
        recv_dk.reshape(owners * CAP, KBS * DH),
        precision=lax.Precision.HIGHEST,
        preferred_element_type=jnp.float32,
    ).reshape(KV_DEV, DH)
    total_dv = jnp.dot(
        block_match,
        recv_dv.reshape(owners * CAP, KBS * DH),
        precision=lax.Precision.HIGHEST,
        preferred_element_type=jnp.float32,
    ).reshape(KV_DEV, DH)
    spread_dk = group_onehot[:, None, None] * total_dk[None, :, :]
    spread_dv = group_onehot[:, None, None] * total_dv[None, :, :]
    grad_keys, grad_values = (
        lax.psum_scatter(
            spread_dk.astype(jnp.bfloat16), "head", scatter_dimension=1, tiled=True
        ).astype(jnp.float32),
        lax.psum_scatter(
            spread_dv.astype(jnp.bfloat16), "head", scatter_dimension=1, tiled=True
        ).astype(jnp.float32),
    )
    return (grad_query, grad_keys.astype(jnp.bfloat16), grad_values.astype(jnp.bfloat16))


def solution(mesh):
    return jax.shard_map(
        body,
        mesh=mesh,
        in_specs=(
            P("ctx", "head", None),
            P(None, "ctx", None),
            P(None, "ctx", None),
            P("ctx", "head", None),
            P(None, "ctx", None),
            P(None, "ctx"),
        ),
        out_specs=(
            P("ctx", "head", None),
            P(None, ("ctx", "head"), None),
            P(None, ("ctx", "head"), None),
        ),
        check_vma=False,
    )
```

profile of v0, /device:TPU:32, one launch (start us, length us, event | category | flops | bytes accessed | tf_op | source)
XLA Modules:
  0.0 595.3 jit_solution(974122711553911189)
XLA Ops:
  7.2 0.9 dynamic-slice_reduce_fusion
  8.2 0.1 lt.77
  8.3 0.1 lt.76
  8.4 0.7 constant_dynamic-slice_fusion.1
  9.0 0.1 reshape.221
  9.1 0.1 reshape.220
  9.3 0.2 select_reduce_fusion
  9.5 0.7 scatter_custom_fusion
  10.2 0.7 all_to_all.20
  10.9 4.3 all-to-all-start
  15.2 1.7 constant_dynamic-slice_fusion
  16.9 0.5 reshape.225
  17.4 0.5 reshape.219
  17.9 2.5 all-to-all-done
  20.5 1.2 gather_fusion.2
  21.7 1.2 gather_fusion
  23.0 1.2 bitcast_select_fusion.4
  24.2 18.5 %all_to_all.32 = bf16[8,8,8192]{2,1,0:T(8,128)(2,1)S(1)} all-to-all(bf16[8,8,8192]{2,1,0:T(8,128)(2,1)S(1)} %get-tuple-element.13), channel_id=1, replica_groups=mesh['ctx'=8,'head'=32] {'ctx'}, dimensions={0} | all-to-all | bytes 2097152 | tf_op jit(solution)/shard_map/all_to_all | solution.py:53
  42.7 3.6 all-to-all-start.1
  46.4 0.1 broadcast_in_dim.62
  46.5 0.1 copy.33
  46.7 1.7 gather_fusion.3
  48.4 13.8 %all-to-all-done.1 = bf16[8,8,8192]{2,1,0:T(8,128)(2,1)S(1)} async-done(((bf16[8,8,8192]{2,1,0:T(8,128)(2,1)}), bf16[8,8,8192]{2,1,0:T(8,128)(2,1)S(1)}, u32[]{:S(2)}, u32[]{:S(2)}) %all-to-all-start.1) | async-done | bytes 1048608 | tf_op jit(solution)/shard_map/all_to_all | solution.py:52
  62.1 1.7 gather_fusion.1
  63.8 1.2 broadcast_select_fusion
  65.0 0.2 reshape.309
  65.3 0.2 reshape.227
  65.5 0.2 reshape.308
  65.8 0.7 fusion.25
  66.5 1.5 fusion.39
  68.0 0.4 fusion.11
  68.4 0.5 fusion.12
  68.9 1.1 copy-done.3
  69.9 0.7 convolution_bitcast_fusion
  70.6 1.2 reshape.286
  71.8 0.1 multiply_reduce_fusion
  71.9 2.9 fusion.3
  74.8 1.4 copy-done.1
  76.2 0.7 convolution_bitcast_fusion.1
  76.9 1.2 reshape.278
  78.1 2.4 scatter_custom_fusion.1
  80.5 3.3 scatter_custom_fusion.2
  83.8 2.7 convert_bitcast_fusion
  86.5 4.2 all-to-all-start.4
  90.7 1.1 convert_bitcast_fusion.1
  91.8 14.8 %all-to-all-done.4 = bf16[8,8,8192]{2,1,0:T(8,128)(2,1)} async-done(((bf16[8,8,8192]{2,1,0:T(8,128)(2,1)}), bf16[8,8,8192]{2,1,0:T(8,128)(2,1)}, u32[]{:S(2)}, u32[]{:S(2)}) %all-to-all-start.4) | async-done | bytes 1048608 | tf_op jit(solution)/shard_map/all_to_all | solution.py:116
  106.6 4.2 all-to-all-start.3
  110.9 0.2 reduce-scatter.5.cloned.1.call-start
  111.1 0.5 broadcast.186
  111.7 0.7 reduce.5
  112.4 3.0 fusion.14
  115.4 1.7 mul.77
  117.1 9.7 %all-to-all-done.3 = bf16[8,8,8192]{2,1,0:T(8,128)(2,1)} async-done(((bf16[8,8,8192]{2,1,0:T(8,128)(2,1)}), bf16[8,8,8192]{2,1,0:T(8,128)(2,1)}, u32[]{:S(2)}, u32[]{:S(2)}) %all-to-all-start.3) | async-done | bytes 1048608 | tf_op jit(solution)/shard_map/all_to_all | solution.py:113
  126.8 3.0 fusion.16
  129.8 2.7 mul.74
  132.5 6.2 %multiply_convert_fusion = (bf16[4,4096,128]{2,1,0:T(8,128)(2,1)}, bf16[4,4096,128]{2,1,0:T(8,128)(2,1)}) fusion(f32[4096,128]{1,0:T(8,128)S(1)} %mul.77, f32[4]{0:T(128)S(1)} %compare_convert_fusion, f32[4096,128]{1,0:T(8,128)} %mul.74), kind=kLoop, calls=%fused_computation.8 | loop fusion | flops 8388608 | bytes 12582928 | tf_op jit(solution)/shard_map/convert_element_type | solution.py:139
  138.8 0.7 reduce-scatter.3.cloned.1.call-update
  139.5 0.2 reshape.223
  139.8 0.6 copy-done.2
  140.3 0.5 fusion.13
  140.8 0.2 copy.38
  141.0 1.0 copy.41
  142.0 220.3 %reduce-scatter.5.cloned.1.call-done = bf16[4,128,128]{2,1,0:T(8,128)(2,1)} async-done(((bf16[4,4096,128]{2,1,0:T(8,128)(2,1)}), bf16[4,128,128]{2,1,0:T(8,128)(2,1)}) %reduce-scatter.5.cloned.1.call-update) | async-done | bytes 131088 | tf_op jit(solution)/shard_map/reduce_scatter | solution.py:138
  362.3 226.1 %reduce-scatter.3.cloned.1.call-done = bf16[4,128,128]{2,1,0:T(8,128)(2,1)} async-done(((bf16[4,4096,128]{2,1,0:T(8,128)(2,1)}), bf16[4,128,128]{2,1,0:T(8,128)(2,1)}) %reduce-scatter.3.cloned.1.call-update) | async-done | bytes 131088 | tf_op jit(solution)/shard_map/reduce_scatter | solution.py:135
  (26 shorter events, 0.6 us)
Async XLA Ops:
  7.2 58.6 %copy-start = (bf16[512,2,128]{2,1,0:T(2,128)(2,1)S(1)}, bf16[512,2,128]{2,1,0:T(2,128)(2,1)}, u32[]{:S(2)}) copy-start(bf16[512,2,128]{2,1,0:T(2,128)(2,1)} %param.10) | copy-start | bytes 786436
  10.9 9.5 %all-to-all-start = ((s32[8,1,8]{2,1,0:T(1,128)}), s32[8,1,8]{2,1,0:T(1,128)S(1)}, u32[]{:S(2)}, u32[]{:S(2)}) async-start(s32[8,1,8]{2,1,0:T(1,128)} %bitcast.2), calls=%async_computation | async-start | bytes 8192 | tf_op jit(solution)/shard_map/all_to_all | solution.py:49
  24.2 22.2 %copy-start.5 = (bf16[512,2,128]{2,1,0:T(2,128)(2,1)S(1)}, bf16[512,2,128]{2,1,0:T(2,128)(2,1)}, u32[]{:S(2)}) copy-start(bf16[512,2,128]{2,1,0:T(2,128)(2,1)} %param.13) | copy-start | bytes 786436
  42.7 19.4 %all-to-all-start.1 = ((bf16[8,8,8192]{2,1,0:T(8,128)(2,1)}), bf16[8,8,8192]{2,1,0:T(8,128)(2,1)S(1)}, u32[]{:S(2)}, u32[]{:S(2)}) async-start(bf16[8,8,8192]{2,1,0:T(8,128)(2,1)} %get-tuple-element.14), calls=%async_computation.1 | async-start | bytes 2097152 | tf_op jit(solution)/shard_map/all_to_all | solution.py:52
  48.4 15.4 %copy-start.4 = (bf16[32,8192]{1,0:T(8,128)(2,1)S(1)}, bf16[32,8192]{1,0:T(8,128)(2,1)}, u32[]{:S(2)}) copy-start(bf16[32,8192]{1,0:T(8,128)(2,1)} %gather_fusion.3) | copy-start | bytes 1572868
  68.0 1.9 copy-start.3
  74.8 1.4 copy-start.1
  86.5 20.2 %all-to-all-start.4 = ((bf16[8,8,8192]{2,1,0:T(8,128)(2,1)}), bf16[8,8,8192]{2,1,0:T(8,128)(2,1)}, u32[]{:S(2)}, u32[]{:S(2)}) async-start(bf16[8,8,8192]{2,1,0:T(8,128)(2,1)} %convert_bitcast_fusion), calls=%async_computation.5 | async-start | bytes 2097152 | tf_op jit(solution)/shard_map/all_to_all | solution.py:116
  106.6 20.2 %all-to-all-start.3 = ((bf16[8,8,8192]{2,1,0:T(8,128)(2,1)}), bf16[8,8,8192]{2,1,0:T(8,128)(2,1)}, u32[]{:S(2)}, u32[]{:S(2)}) async-start(bf16[8,8,8192]{2,1,0:T(8,128)(2,1)} %convert_bitcast_fusion.1), calls=%async_computation.3 | async-start | bytes 2097152 | tf_op jit(solution)/shard_map/all_to_all | solution.py:113
  110.9 251.4 %reduce-scatter.5.cloned.1.call-start = ((), (), s32[]{:S(2)}) async-start(), calls=%async_computation.8 | async-start | bytes 4325376 | tf_op jit(solution)/shard_map/reduce_scatter | solution.py:138
  138.7 1.6 copy-start.2
  138.8 449.7 %reduce-scatter.3.cloned.1.call-start = ((), (), s32[]{:S(2)}) async-start(), calls=%async_computation.7 | async-start | bytes 4325376 | tf_op jit(solution)/shard_map/reduce_scatter | solution.py:135
Sparse Core Ops, SparseCore 0:
  138.9 223.3 reduce-scatter.4
  366.8 221.6 reduce-scatter.2
where the time goes:
time: 597 us; the launch traced here: 595 us
  waiting for transfers between devices  488 us (82%)
  local copies, waits for them, and re-layouts  30.3 us (5%)
  blocking collectives  18.5 us (3%)
  starting transfers between devices  16.6 us (3%)
  other arithmetic  15.5 us (3%)
  between operations  14.3 us (2%)
  matrix products  12.1 us (2%)
    reduce_scatter x1, waiting for transfers between devices, body(): lax.psum_scatter(spread_dk.astype(jnp.bfloat16), 'head', scatter_dimensio...  226 us
    reduce_scatter x1, waiting for transfers between devices, body(): lax.psum_scatter(spread_dv.astype(jnp.bfloat16), 'head', scatter_dimensio...  220 us
    all_to_all x1, blocking collectives, body(): lax.all_to_all(value_rows, 'ctx', split_axis=0, concat_axis=0, tiled=True)  18.5 us
    all_to_all x1, waiting for transfers between devices, body(): lax.all_to_all(home_dv.astype(jnp.bfloat16), 'ctx', split_axis=0, concat_...  14.8 us
    all_to_all x1, waiting for transfers between devices, body(): lax.all_to_all(key_rows, 'ctx', split_axis=0, concat_axis=0, tiled=True)  13.8 us
  transfers between devices with their start and end apart: 6, of which 6 were waited for; matrix products, arithmetic and copies ran while one was open for 2% of the time, Pallas kernels for 0%

commit v1 on v0

v1 whole, which is shorter than its diff:
```python
import jax
import jax.numpy as jnp
from jax import lax
from jax.experimental import pallas as pl
from jax.experimental.pallas import tpu as pltpu
from jax.sharding import Mesh
from jax.sharding import PartitionSpec as P

DH = 128
KBS = 64
TOPB = 16
BLK_OWN = 64
CAP = 8
OWN = 8
PIECE = 16
GROUPS = 4
ROWS = 1024
TILE = 256
QKEYS = 256
INV_ROOT = DH ** (-0.5)
LOG2E = 1.4426950408889634

BF = jnp.bfloat16
F32 = jnp.float32
I32 = jnp.int32
SMEM = pltpu.MemorySpace.SMEM
VMEM = pltpu.MemorySpace.VMEM


def request_kernel(place, chosen, counts, requests, meta, fill):
    group = place[0]
    for o in range(OWN):
        fill[o] = 0
        for r in range(CAP):
            requests[o, r] = 0
    for b in range(2):
        live_count = counts[group, b]
        meta[2 * TOPB + b] = live_count

        def visit(t, carry, b=b, live_count=live_count):
            block = chosen[group, b, t]
            owner = block // BLK_OWN

            @pl.when(t < live_count)
            def _():
                rank = fill[owner]
                requests[owner, rank] = block % BLK_OWN
                fill[owner] = rank + 1
                meta[b * TOPB + t] = owner * CAP + rank

            @pl.when(t >= live_count)
            def _():
                meta[b * TOPB + t] = meta[b * TOPB]

            return carry

        lax.fori_loop(0, TOPB, visit, 0)


def gather_kernel(place, asked, keys, values, out, sem):
    group = place[0]
    first = place[2] * PIECE

    def copy_from(source):
        def visit(n, carry):
            block = asked[n // CAP, n % CAP]
            pltpu.make_async_copy(
                source.at[group, pl.ds(block * KBS + first, PIECE), :], out.at[n], sem
            ).start()
            return carry

        lax.fori_loop(0, OWN * CAP, visit, 0, unroll=8)

    @pl.when(place[1] == 0)
    def _():
        copy_from(keys)

    @pl.when(place[1] != 0)
    def _():
        copy_from(values)

    pltpu.make_async_copy(out, out, sem).wait()


def compact_kernel(meta, got, out):
    for b in range(2):

        def visit(t, carry, b=b):
            tile = got[meta[b * TOPB + t]]
            for a in range(4):
                out[2 * a + b, t] = tile
            return carry

        lax.fori_loop(0, TOPB, visit, 0, unroll=4)


def attention_kernel(meta, place, kv, query, grad, dq, dkv, kt, vt, acc, prob, half):
    step = pl.program_id(0)

    @pl.when(step == 0)
    def _():
        for n in range(4):
            cols = pl.ds(n * QKEYS, QKEYS)
            kt[:, cols] = kv[n].T
            vt[:, cols] = kv[4 + n].T
        acc[...] = jnp.zeros_like(acc)

    live_rows = meta[2 * TOPB + place[3]] * PIECE
    row = lax.broadcasted_iota(I32, (QKEYS, TILE), 0)
    live = row < live_rows
    q = query[...]
    g = grad[...]
    nt = (((1,), (1,)), ((), ()))
    peak = jnp.full((1, TILE), -jnp.inf, F32)
    for n in range(4):
        s = lax.dot_general(kv[n], q, nt, preferred_element_type=F32)
        s = jnp.where(live, s, -jnp.inf)
        prob[n] = s
        peak = jnp.maximum(peak, jnp.max(s, axis=0, keepdims=True))
    scale = INV_ROOT * LOG2E
    total = jnp.zeros((1, TILE), F32)
    for n in range(4):
        p = jnp.exp2((prob[n] - peak) * scale)
        prob[n] = p
        total = total + jnp.sum(p, axis=0, keepdims=True)
    rate = 1.0 / total
    out_t = jnp.zeros((DH, TILE), F32)
    for n in range(4):
        w = prob[n] * rate
        prob[n] = w
        wh = w.astype(BF)
        half[n] = wh
        out_t = out_t + jnp.dot(
            vt[:, n * QKEYS : (n + 1) * QKEYS], wh, preferred_element_type=F32
        )
    g_t = g.astype(F32).T
    row_dot = jnp.sum(g_t * out_t.astype(BF).astype(F32), axis=0, keepdims=True)
    dq_t = jnp.zeros((DH, TILE), F32)
    for n in range(4):
        gw = lax.dot_general(kv[4 + n], g, nt, preferred_element_type=F32)
        ds = (prob[n] * (gw - row_dot) * INV_ROOT).astype(BF)
        dq_t = dq_t + jnp.dot(
            kt[:, n * QKEYS : (n + 1) * QKEYS], ds, preferred_element_type=F32
        )
        acc[n] += jnp.dot(ds, q, preferred_element_type=F32)
        acc[4 + n] += jnp.dot(half[n], g, preferred_element_type=F32)
    dq[...] = dq_t.T.astype(BF)

    @pl.when(step == pl.num_programs(0) - 1)
    def _():
        dkv[...] = acc[...].astype(BF)


def home_kernel(meta, parts, out):
    out[...] = jnp.zeros_like(out)
    for b in range(2):

        def visit(t, carry, b=b):
            @pl.when(t < meta[2 * TOPB + b])
            def _():
                tile = parts[b, t].astype(F32)
                for a in range(1, 4):
                    tile = tile + parts[2 * a + b, t].astype(F32)
                out[meta[b * TOPB + t]] = tile.astype(BF)

            return carry

        lax.fori_loop(0, TOPB, visit, 0)


def block_kernel(asked, parts, out, acc):
    acc[...] = jnp.zeros_like(acc)

    def visit(n, carry):
        block = asked[n // CAP, n % CAP]
        acc[block] = acc[block] + parts[n].astype(F32)
        return carry

    lax.fori_loop(0, OWN * CAP, visit, 0, unroll=8)
    out[...] = acc[...].astype(BF)


def place_kernel(parts, grad_keys, grad_values):
    for g in range(GROUPS):
        for part in range(4):
            for e in range(2):
                rows = pl.ds(e * KBS + part * PIECE, PIECE)
                grad_keys[g, rows, :] = parts[g * 8 + part, e]
                grad_values[g, rows, :] = parts[g * 8 + 4 + part, e]


def shape(dims, dtype=BF):
    return jax.ShapeDtypeStruct(dims, dtype)


def whole(space=VMEM):
    return pl.BlockSpec(memory_space=space)


def call(kernel, out_shape, in_specs, out_specs, scratch=(), name=None):
    return pl.pallas_call(
        kernel,
        out_shape=out_shape,
        in_specs=in_specs,
        out_specs=out_specs,
        scratch_shapes=scratch,
        name=name,
    )


def exchange(x, axes):
    return lax.all_to_all(x, axes, split_axis=0, concat_axis=0, tiled=True)


def body(queries, cached_keys, cached_values, grad_out, chosen, counts):
    zb = lax.axis_index("zb")
    z = lax.axis_index(("za", "zb"))
    place = jnp.stack([lax.axis_index("y"), z // 4, z % 4, zb]).astype(I32)
    ring = ("za", "zb")
    query_rows = exchange(queries.reshape(ROWS, DH), "zb")
    grad_rows = exchange(grad_out.reshape(ROWS, DH), "zb")
    requests, meta = call(
        request_kernel,
        (shape((OWN, CAP), I32), shape((2 * TOPB + 2,), I32)),
        [whole(SMEM)] * 3,
        (whole(SMEM),) * 2,
        [pltpu.SMEM((OWN,), I32)],
        name="request",
    )(place, chosen, counts)
    asked = exchange(requests, "ctx")
    pieces = call(
        gather_kernel,
        shape((OWN * CAP, PIECE, DH)),
        [whole(SMEM)] * 2 + [whole(pl.ANY)] * 2,
        whole(pl.ANY),
        [pltpu.SemaphoreType.DMA],
        name="gather",
    )(place, asked, cached_keys, cached_values)
    fetched = exchange(pieces, "ctx")
    spread = call(
        compact_kernel,
        shape((8, TOPB, PIECE, DH)),
        [whole(SMEM), whole()],
        whole(),
        name="compact",
    )(meta, fetched)
    kv = exchange(spread, ring).reshape(8, QKEYS, DH)
    tiles = pl.BlockSpec((TILE, DH), lambda i: (i, 0))
    fixed = pl.BlockSpec((8, QKEYS, DH), lambda i: (0, 0, 0))
    dq_rows, slot_grads = pl.pallas_call(
        attention_kernel,
        grid=(ROWS // TILE,),
        out_shape=(shape((ROWS, DH)), shape((8, QKEYS, DH))),
        in_specs=[whole(SMEM), whole(SMEM), fixed, tiles, tiles],
        out_specs=(tiles, fixed),
        scratch_shapes=[
            pltpu.VMEM((DH, ROWS), BF),
            pltpu.VMEM((DH, ROWS), BF),
            pltpu.VMEM((8, QKEYS, DH), F32),
            pltpu.VMEM((4, QKEYS, TILE), F32),
            pltpu.VMEM((4, QKEYS, TILE), BF),
        ],
        name="attention",
    )(meta, place, kv, query_rows, grad_rows)
    grad_query = exchange(dq_rows, "zb").reshape(queries.shape)
    parts = exchange(slot_grads, ring).reshape(8, TOPB, PIECE, DH)
    home = call(
        home_kernel,
        shape((OWN * CAP, PIECE, DH)),
        [whole(SMEM), whole()],
        whole(),
        name="home",
    )(meta, parts)
    arrived = exchange(home, "ctx")
    block_sums = call(
        block_kernel,
        shape((BLK_OWN, PIECE, DH)),
        [whole(SMEM), whole()],
        whole(),
        [pltpu.VMEM((BLK_OWN, PIECE, DH), F32)],
        name="blocks",
    )(asked, arrived)
    placed = exchange(block_sums, ("y",) + ring).reshape(32, 2, PIECE, DH)
    grad_keys, grad_values = call(
        place_kernel,
        (shape((GROUPS, 2 * KBS, DH)),) * 2,
        [whole()],
        (whole(),) * 2,
        name="place",
    )(placed)
    return grad_query, grad_keys, grad_values


def solution(mesh):
    fine = Mesh(mesh.devices.reshape(8, 4, 4, 2), ("ctx", "y", "za", "zb"))
    head = ("y", "za", "zb")
    return jax.shard_map(
        body,
        mesh=fine,
        in_specs=(
            P("ctx", head, None),
            P(None, "ctx", None),
            P(None, "ctx", None),
            P("ctx", head, None),
            P(None, "ctx", None),
            P(None, "ctx"),
        ),
        out_specs=(
            P("ctx", head, None),
            P(None, ("ctx",) + head, None),
            P(None, ("ctx",) + head, None),
        ),
        check_vma=False,
    )
```

time: 597 us -> 145 us (0.24)
  waiting for transfers between devices: 488 us -> 13.5 us
  blocking collectives: 18.5 us -> 80.2 us
  Pallas kernels: 0 us -> 29.3 us
  local copies, waits for them, and re-layouts: 30.3 us -> 2.75 us
  other arithmetic: 15.5 us -> 0.67 us
  between operations: 14.3 us -> 0.69 us
  matrix products: 12.1 us -> 0 us
    reduce_scatter x2 -> x0, waiting for transfers between devices: 446 us -> none  [the longest x1 226 us: body(): lax.psum_scatter(spread_dk.astype(jnp.bfloat16), 'head', scatter_dimensio...]
    all_to_all x1 -> x6, blocking collectives: 18.5 us -> 80.2 us  [exchange(): return lax.all_to_all(x, axes, split_axis=0, concat_axis=0, tiled=True)]
    pallas_call x0 -> x7, Pallas kernels: none -> 29.3 us  [the longest x1 9.94 us: body(): call(gather_kernel, shape((OWN * CAP, PIECE, DH)), [whole(SMEM)] * 2 + [w...]
    all_to_all x4 -> x3, waiting for transfers between devices: 40.8 us -> 13.5 us  [exchange(): return lax.all_to_all(x, axes, split_axis=0, concat_axis=0, tiled=True)]
    dot_general x8 -> x0, matrix products: 12.1 us -> none  [the longest x1 3 us: body(): jnp.dot(block_match, recv_dv.reshape(owners * CAP, KBS * DH), precision=l...]
    convert_element_type x6 -> x0, other arithmetic: 10.4 us -> none  [the longest x1 6.23 us: body(): spread_dv.astype(jnp.bfloat16)]
    scatter x3 -> x0, local copies, waits for them, and re-layouts: 6.32 us -> none  [the longest x1 3.29 us: body(): home_dv = jnp.zeros((owners * CAP, KBS * DH), jnp.float32).at[target].set...]
    all_to_all x4 -> x3, starting transfers between devices: 16.3 us -> 16.9 us  [exchange(): return lax.all_to_all(x, axes, split_axis=0, concat_axis=0, tiled=True)]
  transfers between devices with their start and end apart: 6 -> 3, of which waited for: 6 -> 3; matrix products, arithmetic and copies ran while one was open for 2% -> 0% of each run, Pallas kernels for 0% -> 3%
where the time goes in v1:
time: 145 us; the launch traced here: 144 us
  blocking collectives  80.2 us (55%)
  Pallas kernels  29.3 us (20%)
  starting transfers between devices  16.9 us (12%)
  waiting for transfers between devices  13.5 us (9%)
  local copies, waits for them, and re-layouts  2.75 us (2%)
    all_to_all x6, blocking collectives, exchange(): return lax.all_to_all(x, axes, split_axis=0, concat_axis=0, tiled=True)  80.2 us
    all_to_all x3, starting transfers between devices, exchange(): return lax.all_to_all(x, axes, split_axis=0, concat_axis=0, tiled=True)  16.9 us
    all_to_all x3, waiting for transfers between devices, exchange(): return lax.all_to_all(x, axes, split_axis=0, concat_axis=0, tiled=True)  13.5 us
    pallas_call x1, Pallas kernels, body(): call(gather_kernel, shape((OWN * CAP, PIECE, DH)), [whole(SMEM)] * 2 + [w...  9.94 us
    pallas_call x1, Pallas kernels, body(): pl.pallas_call(attention_kernel, grid=(ROWS // TILE,), out_shape=(shape((...  9.13 us
  transfers between devices with their start and end apart: 3, of which 3 were waited for; matrix products, arithmetic and copies ran while one was open for 0% of the time, Pallas kernels for 3%

profile of v1, /device:TPU:32, one launch (start us, length us, event | category | flops | bytes accessed | tf_op | source)
XLA Modules:
  0.0 144.0 jit_solution(5940788640541022658)
XLA Ops:
  0.7 1.3 copy.10.counts
  2.0 0.7 pad_add_fusion.place
  2.7 2.1 %request.1 = (s32[8,8]{1,0:T(8,128)}, s32[34]{0:T(128)}) custom-call(s32[4]{0:T(128)} %pad_add_fusion.place, s32[4,2,16]{2,1,0:T(2,128)} %chosen.1, s32[4,2]{1,0:T(4,128)} %copy.10.counts), custom_call_target="tpu_custom_call" | custom-call | tf_op jit(solution)/shard_map/request/pallas_call | solution.py:222
  4.8 9.5 %all_to_all.67 = s32[8,1,8]{2,1,0:T(1,128)} all-to-all(s32[8,1,8]{2,1,0:T(1,128)} %bitcast.27), channel_id=1, replica_groups=mesh['ctx'=8,'y'=4,'za'=4,'zb'=2] {'ctx'}, dimensions={0} | all-to-all | bytes 512 | tf_op jit(solution)/shard_map/all_to_all | solution.py:212
  14.3 0.0 copy-start.2
  14.3 9.9 %gather.1 = bf16[64,16,128]{2,1,0:T(8,128)(2,1)} custom-call(s32[4]{0:T(128)} %pad_add_fusion.place, s32[8,8]{1,0:T(8,128)} %bitcast.25, bf16[4,4096,128]{2,1,0:T(8,128)(2,1)} %keys.1, bf16[4,4096,128]{2,1,0:T(8,128)(2,1)} %values.1), custom_call_target="tpu_custom_call" | custom-call | tf_op jit(solution)/shard_map/gather/pallas_call | solution.py:231
  24.2 11.5 %all_to_all.68.got = bf16[64,16,128]{2,1,0:T(8,128)(2,1)} all-to-all(bf16[64,16,128]{2,1,0:T(8,128)(2,1)} %gather.1), channel_id=1, replica_groups=mesh['ctx'=8,'y'=4,'za'=4,'zb'=2] {'ctx'}, dimensions={0} | all-to-all | bytes 524288 | tf_op jit(solution)/shard_map/all_to_all | solution.py:212
  35.8 0.0 copy-done.2
  35.8 7.7 %all_to_all.69 = bf16[2,512,128]{2,1,0:T(8,128)(2,1)} all-to-all(bf16[2,512,128]{2,1,0:T(8,128)(2,1)S(1)} %bitcast.23), channel_id=1, replica_groups=mesh['ctx'=8,'y'=4,'za'=4,'zb'=2] {'zb'}, dimensions={0} | all-to-all | bytes 524288 | tf_op jit(solution)/shard_map/all_to_all | solution.py:212
  43.5 5.3 %all-to-all-start.4 = ((bf16[2,512,128]{2,1,0:T(8,128)(2,1)}), bf16[2,512,128]{2,1,0:T(8,128)(2,1)S(1)}, u32[]{:S(2)}, u32[]{:S(2)}) async-start(bf16[2,512,128]{2,1,0:T(8,128)(2,1)} %bitcast.10), calls=%async_computation.4 | async-start | bytes 524288 | tf_op jit(solution)/shard_map/all_to_all | solution.py:212
  48.7 1.9 %compact.1 = bf16[8,16,16,128]{3,2,1,0:T(8,128)(2,1)} custom-call(s32[34]{0:T(128)} %get-tuple-element.9.meta, bf16[64,16,128]{2,1,0:T(8,128)(2,1)} %all_to_all.68.got), custom_call_target="tpu_custom_call" | custom-call | tf_op jit(solution)/shard_map/compact/pallas_call | solution.py:240
  50.6 1.3 all-to-all-done.4
  51.9 0.0 copy-start
  51.9 22.8 %all_to_all.70 = bf16[8,16,16,128]{3,2,1,0:T(8,128)(2,1)} all-to-all(bf16[8,16,16,128]{3,2,1,0:T(8,128)(2,1)} %compact.1), channel_id=1, replica_groups=mesh['ctx'=8,'y'=4,'za'=4,'zb'=2] {'za','zb'}, dimensions={0} | all-to-all | bytes 1048576 | tf_op jit(solution)/shard_map/all_to_all | solution.py:212
  74.7 0.0 copy-done
  74.7 9.1 %attention.1 = (bf16[1024,128]{1,0:T(8,128)(2,1)}, bf16[8,256,128]{2,1,0:T(8,128)(2,1)}) custom-call(s32[34]{0:T(128)} %get-tuple-element.9.meta, s32[4]{0:T(128)} %pad_add_fusion.place, bf16[8,256,128]{2,1,0:T(8,128)(2,1)} %bitcast.17, bf16[1024,128]{1,0:T(8,128)(2,1)} %bitcast.19, bf16[1024,128]{1,0:T(8,128)(2,1)} %bitcast.20), custom_call_target="tpu_custom_call" | custom-call | tf_op jit(solution)/shard_map/attention/pallas_call | solution.py:250
  83.8 17.1 %all_to_all.71 = bf16[8,256,128]{2,1,0:T(8,128)(2,1)} all-to-all(bf16[8,256,128]{2,1,0:T(8,128)(2,1)} %get-tuple-element.12), channel_id=1, replica_groups=mesh['ctx'=8,'y'=4,'za'=4,'zb'=2] {'za','zb'}, dimensions={0} | all-to-all | bytes 1048576 | tf_op jit(solution)/shard_map/all_to_all | solution.py:212
  100.9 2.3 %home.1 = bf16[64,16,128]{2,1,0:T(8,128)(2,1)} custom-call(s32[34]{0:T(128)} %get-tuple-element.9.meta, bf16[8,16,16,128]{3,2,1,0:T(8,128)(2,1)} %bitcast.18), custom_call_target="tpu_custom_call" | custom-call | tf_op jit(solution)/shard_map/home/pallas_call | solution.py:267
  103.2 11.6 %all_to_all.72.parts = bf16[64,16,128]{2,1,0:T(8,128)(2,1)} all-to-all(bf16[64,16,128]{2,1,0:T(8,128)(2,1)} %home.1), channel_id=1, replica_groups=mesh['ctx'=8,'y'=4,'za'=4,'zb'=2] {'ctx'}, dimensions={0} | all-to-all | bytes 524288 | tf_op jit(solution)/shard_map/all_to_all | solution.py:212
  114.8 5.2 %all-to-all-start.5 = ((bf16[2,512,128]{2,1,0:T(8,128)(2,1)}), bf16[2,512,128]{2,1,0:T(8,128)(2,1)S(1)}, u32[]{:S(2)}, u32[]{:S(2)}) async-start(bf16[2,512,128]{2,1,0:T(8,128)(2,1)} %bitcast.24), calls=%async_computation.5 | async-start | bytes 524288 | tf_op jit(solution)/shard_map/all_to_all | solution.py:212
  119.9 2.3 %blocks.1 = bf16[64,16,128]{2,1,0:T(8,128)(2,1)} custom-call(s32[8,8]{1,0:T(8,128)} %bitcast.26, bf16[64,16,128]{2,1,0:T(8,128)(2,1)} %all_to_all.72.parts), custom_call_target="tpu_custom_call" | custom-call | tf_op jit(solution)/shard_map/blocks/pallas_call | solution.py:275
  122.2 1.1 all-to-all-done.5
  123.3 6.5 %all-to-all-start.8 = ((bf16[64,16,128]{2,1,0:T(8,128)(2,1)}), bf16[64,16,128]{2,1,0:T(8,128)(2,1)S(1)}, u32[]{:S(2)}, u32[]{:S(2)}) async-start(bf16[64,16,128]{2,1,0:T(8,128)(2,1)} %blocks.1), calls=%async_computation.8 | async-start | bytes 524288 | tf_op jit(solution)/shard_map/all_to_all | solution.py:212
  129.7 11.1 %all-to-all-done.8 = bf16[64,16,128]{2,1,0:T(8,128)(2,1)S(1)} async-done(((bf16[64,16,128]{2,1,0:T(8,128)(2,1)}), bf16[64,16,128]{2,1,0:T(8,128)(2,1)S(1)}, u32[]{:S(2)}, u32[]{:S(2)}) %all-to-all-start.8) | async-done | bytes 262176 | tf_op jit(solution)/shard_map/all_to_all | solution.py:212
  140.9 0.0 copy-start.1
  140.9 0.7 copy-done.1
  141.6 1.7 %place.1 = (bf16[4,128,128]{2,1,0:T(8,128)(2,1)}, bf16[4,128,128]{2,1,0:T(8,128)(2,1)}) custom-call(bf16[32,2,16,128]{3,2,1,0:T(8,128)(2,1)} %bitcast.22), custom_call_target="tpu_custom_call" | custom-call | tf_op jit(solution)/shard_map/place/pallas_call | solution.py:284
  143.3 0.7 copy.13
Async XLA Ops:
  14.3 21.5 %copy-start.2 = (bf16[512,2,128]{2,1,0:T(2,128)(2,1)S(1)}, bf16[512,2,128]{2,1,0:T(2,128)(2,1)}, u32[]{:S(2)}) copy-start(bf16[512,2,128]{2,1,0:T(2,128)(2,1)} %param.6) | copy-start | bytes 786436
  43.5 8.4 %all-to-all-start.4 = ((bf16[2,512,128]{2,1,0:T(8,128)(2,1)}), bf16[2,512,128]{2,1,0:T(8,128)(2,1)S(1)}, u32[]{:S(2)}, u32[]{:S(2)}) async-start(bf16[2,512,128]{2,1,0:T(8,128)(2,1)} %bitcast.10), calls=%async_computation.4 | async-start | bytes 524288 | tf_op jit(solution)/shard_map/all_to_all | solution.py:212
  51.9 22.8 %copy-start = (bf16[2,512,128]{2,1,0:T(8,128)(2,1)}, bf16[2,512,128]{2,1,0:T(8,128)(2,1)S(1)}, u32[]{:S(2)}) copy-start(bf16[2,512,128]{2,1,0:T(8,128)(2,1)S(1)} %all-to-all-done.4) | copy-start | bytes 786436
  114.8 8.5 %all-to-all-start.5 = ((bf16[2,512,128]{2,1,0:T(8,128)(2,1)}), bf16[2,512,128]{2,1,0:T(8,128)(2,1)S(1)}, u32[]{:S(2)}, u32[]{:S(2)}) async-start(bf16[2,512,128]{2,1,0:T(8,128)(2,1)} %bitcast.24), calls=%async_computation.5 | async-start | bytes 524288 | tf_op jit(solution)/shard_map/all_to_all | solution.py:212
  123.3 17.6 %all-to-all-start.8 = ((bf16[64,16,128]{2,1,0:T(8,128)(2,1)}), bf16[64,16,128]{2,1,0:T(8,128)(2,1)S(1)}, u32[]{:S(2)}, u32[]{:S(2)}) async-start(bf16[64,16,128]{2,1,0:T(8,128)(2,1)} %blocks.1), calls=%async_computation.8 | async-start | bytes 524288 | tf_op jit(solution)/shard_map/all_to_all | solution.py:212
  140.9 0.7 copy-start.1
